TPU v7x, 32 devices: a whole 2x2x4 slice. The times are simulated.
32 devices in a mesh: row: 4 (over z), col: 8 (over y, x, core).
Axes of the slice: x: 2, y: 2, z: 4, core: 2. Of those that a mesh axis runs over, the one named last changes fastest.
Arguments:
- trailing: float32 [16384, 3072], P('row', 'col'), may hold values from -6 to 6
- leaf_vectors: float32 [16384, 256], P(('row', 'col')), may hold values from -1 to 1, as said below
- leaf_factor: float32 [1024, 256], P(('row', 'col')), may hold values from -1 to 2, as said below
- tree_vectors: float32 [1024, 256], P(('row', 'col')), may hold values from -1 to 1, as said below
- tree_factor: float32 [1024, 256], P(('row', 'col')), may hold values from -1 to 2, as said below
Outputs:
- updated: float32 [16384, 3072], P('row', 'col')
Inputs may be any that keep to these rules, and one draw needn't show every extreme that they name: `leaf_vectors`: in each row block of 4096 rows, row r < 256 of the block holds 1 in column r and 0 in every column after r. `leaf_factor`: each 256 x 256 block is upper triangular with its diagonal between 1 and 2. `tree_vectors`: each 256 x 256 block is upper triangular. `tree_factor`: each 256 x 256 block is upper triangular with its diagonal between 1 and 2.
All inputs are finite; a program needn't handle non-finite values.
Results may differ from a plain program's by a relative error of at most 0.0002.
Values sent between devices are 32-bit elements; how exact they have to be, the bound alone decides.
No kernel may reach another device: no remote copies, remote signals or barrier semaphores. Data moves between devices by JAX's collectives and lax.ppermute only.
A program may use at most 128 MiB of HBM per device.

v0:
```python
import math

import jax
import jax.numpy as jnp
from jax import lax
from jax.experimental import pallas as pl
from jax.experimental.pallas import tpu as pltpu
from jax.sharding import PartitionSpec as P


ROWS = (((0,), (0,)), ((), ()))
PLAIN = (((1,), (0,)), ((), ()))
HBM = pl.BlockSpec(memory_space=pltpu.HBM)
WHOLE = pl.BlockSpec(memory_space=pltpu.VMEM)
GRANT = 4 << 20
PARTS = 8
TILES = 6


def halves(array):
    high = array.astype(jnp.bfloat16)
    return high, (array - high.astype(jnp.float32)).astype(jnp.bfloat16)


def narrow(first, second, dims):
    return lax.dot_general(first, second, dims, preferred_element_type=jnp.float32)


def product(first, second, dims):
    first_high, first_low = halves(first)
    second_high, second_low = halves(second)
    return narrow(first_high, second_high, dims) + (
        narrow(first_high, second_low, dims) + narrow(first_low, second_high, dims)
    )


def thrice(high, low, factor_high, factor_low):
    return narrow(high, factor_high, PLAIN) + (narrow(high, factor_low, PLAIN) + narrow(low, factor_high, PLAIN))


def out(*shape):
    return pltpu.VMEM(shape, jnp.float32)


def outside(*shape):
    return pltpu.HBM(shape, jnp.float32)


def role_of(level):
    stride = 1 << level
    inside = lax.rem(lax.axis_index("row"), 2 * stride)
    return jnp.where(inside == 0, 1, jnp.where(inside == stride, 2, 0))


def outer(*arrays):
    return tuple(pltpu.with_memory_space_constraint(array, pltpu.HBM) for array in arrays)


def exchanged(array, mask):
    return lax.ppermute(array, "col", [(i, i ^ mask) for i in range(lax.axis_size("col"))])


def kernel_call(kernel, arguments, flops, moved, grant=GRANT, **options):
    return pl.pallas_call(
        kernel,
        compiler_params=pltpu.CompilerParams(vmem_limit_bytes=grant),
        cost_estimate=pl.CostEstimate(flops=flops, bytes_accessed=moved, transcendentals=0),
        **options,
    )(*arguments)


def pack(leaf_vectors, leaf_factor, tree_vectors, tree_factor, ranges):
    tall, short = leaf_vectors.shape[0], leaf_factor.shape[0]
    parts = len(ranges)

    def kernel(vectors_ref, factor_ref, tree_vectors_ref, tree_factor_ref, *refs):
        *part_refs, own_ref, sems = refs
        moves = [(tree_vectors_ref, own_ref.at[pl.ds(0, short)]), (tree_factor_ref, own_ref.at[pl.ds(short, short)])]
        for (start, stop), ref in zip(ranges, part_refs):
            upper = min(stop, tall) - start
            moves.append((vectors_ref.at[pl.ds(start, upper)], ref.at[pl.ds(0, upper)]))
            if stop > tall:
                moves.append((factor_ref, ref.at[pl.ds(upper, short)]))
        copies = [pltpu.make_async_copy(source, target, sems.at[n]) for n, (source, target) in enumerate(moves)]
        for copy in copies:
            copy.start()
        for copy in copies:
            copy.wait()

    width = leaf_vectors.shape[1]
    return kernel_call(
        kernel, outer(leaf_vectors, leaf_factor, tree_vectors, tree_factor), 0, 8 * tall * width,
        in_specs=[HBM] * 4, out_specs=[WHOLE] * (parts + 1),
        out_shape=[out(stop - start, width) for start, stop in ranges] + [out(2 * short, width)],
        scratch_shapes=[pltpu.SemaphoreType.DMA((parts + 3,))],
    )


def load(array):
    rows = array.shape[0] // PARTS

    def kernel(array_ref, out_ref, high_ref, low_ref, sems):
        copies = []
        for n in range(PARTS):
            part = pl.ds(n * rows, rows)
            copies.append(pltpu.make_async_copy(array_ref.at[part], out_ref.at[part], sems.at[n]))
            copies[-1].start()
        for n, copy in enumerate(copies):
            copy.wait()
            part = pl.ds(n * rows, rows)
            high_ref[part, :], low_ref[part, :] = halves(out_ref[part, :])

    shape = array.shape
    return kernel_call(
        kernel, outer(array), 0, 12 * array.size,
        in_specs=[HBM], out_specs=[WHOLE] * 3,
        out_shape=[out(*shape), pltpu.VMEM(shape, jnp.bfloat16), pltpu.VMEM(shape, jnp.bfloat16)],
        scratch_shapes=[pltpu.SemaphoreType.DMA((PARTS,))],
    )


def join(arrays):
    def kernel(*refs):
        start = 0
        for ref in refs[:-1]:
            refs[-1][start : start + ref.shape[0], :] = ref[...]
            start += ref.shape[0]

    rows = sum(array.shape[0] for array in arrays)
    return kernel_call(
        kernel, arrays, 0, 8 * rows * arrays[0].shape[1],
        in_specs=[WHOLE] * len(arrays), out_specs=WHOLE, out_shape=out(rows, arrays[0].shape[1]),
    )


def pick(level, own, sent):
    def kernel(own_ref, sent_ref, out_ref):
        out_ref[...] = jnp.where(role_of(level) == 2, own_ref[...], sent_ref[...])

    return kernel_call(
        kernel, (own, sent), 0, 12 * own.size,
        in_specs=[WHOLE, WHOLE], out_specs=WHOLE, out_shape=out(*own.shape),
    )


def gram(pieces, trailing, tall, short, state, top=None):
    whole, _, _ = trailing
    width, columns = pieces[0][2].shape[1], whole.shape[1]
    rows = whole.shape[0]
    count, begins = len(pieces), state is None

    def kernel(whole_ref, high_ref, lower_ref, *refs):
        piece_refs, refs = refs[:count], refs[count:]
        total_of = None
        if not begins:
            total_of, refs = refs[2][...], refs[3:]
        held_ref, square_ref, total_ref, *refs = refs
        place = lax.axis_index("col")
        for (mask, offset, array), ref in zip(pieces, piece_refs):
            size = array.shape[0]
            block = place ^ mask
            upper = min(size, tall - offset)
            here = pl.ds(pl.multiple_of(block * tall + offset, math.gcd(tall, offset)), upper)
            vectors = jnp.concatenate(halves(ref[:upper, :]), 1)
            held_ref[here, :] = vectors
            term = narrow(vectors, high_ref[here, :], ROWS) + narrow(vectors, lower_ref[here, :], ROWS)
            term = term[:width] + term[width:]
            total_of = term if total_of is None else total_of + term
            if upper < size:
                there = pl.ds(pl.multiple_of(block * short, short), short)
                square_ref[there, :] = ref[upper:, :]
        total_ref[...] = total_of
        if top is not None:
            leading(0, top, whole_ref, held_ref, square_ref, total_of, None, *refs)

    arrays = [piece[2] for piece in pieces]
    taken = sum(array.shape[0] for array in arrays)
    states = () if begins else state
    return kernel_call(
        kernel, (*trailing, *arrays, *states),
        8 * taken * width * columns, 8 * taken * width,
        in_specs=[WHOLE] * (3 + count + len(states)),
        out_specs=[WHOLE] * (3 if top is None else 5),
        out_shape=[pltpu.VMEM((rows, 2 * width), jnp.bfloat16), out(width, width), out(width, columns)]
        + ([] if top is None else [out(top, columns)] * 2),
        input_output_aliases={} if begins else {3 + count: 0, 4 + count: 1},
    )


def leading(low, high, whole_ref, held_ref, square_ref, total, before, weights_ref, top_ref):
    width = square_ref.shape[0]
    weights = product(square_ref[:high, low:high], total[:high], ROWS)
    weights_ref[...] = weights
    if before is not None:
        weights = jnp.concatenate([before, weights], 0)
    vectors = held_ref[low:high, :]
    top_ref[...] = whole_ref[low:high, :] - thrice(vectors[:, :high], vectors[:, width : width + high], *halves(weights))


def weigh(low, high, trailing, held, square, total, before):
    columns = trailing.shape[1]

    def kernel(whole_ref, held_ref, square_ref, total_ref, before_ref, weights_ref, top_ref):
        leading(low, high, whole_ref, held_ref, square_ref, total_ref[...], before_ref[...], weights_ref, top_ref)

    return kernel_call(
        kernel, (trailing, held, square, total, before), 6 * high * high * columns, 8 * high * columns,
        in_specs=[WHOLE] * 5, out_specs=[WHOLE] * 2, out_shape=[out(high - low, columns)] * 2,
    )


def update(trailing, held, weights):
    rows, columns = trailing.shape
    panel = held.shape[1] // 2
    below = rows - panel
    tile = below // TILES if below % (16 * TILES) == 0 else panel
    tiles = below // tile
    chunks = len(weights)

    def kernel(trailing_ref, held_ref, *refs):
        weights_refs, (out_ref, result, factors, sems) = refs[:chunks], refs[chunks:]
        high, low = halves(jnp.concatenate([ref[...] for ref in weights_refs], 0))
        factors[:, :columns] = high
        factors[:, columns:] = low

        def rows_of(n):
            return pl.ds(pl.multiple_of(panel + n * tile, math.gcd(panel, tile)), tile)

        def store(n):
            return pltpu.make_async_copy(result.at[n], out_ref.at[rows_of(n)], sems.at[n])

        @pl.loop(0, tiles)
        def _(n):
            here = rows_of(n)
            both = narrow(held_ref[here, :panel], factors[...], PLAIN)
            rest = narrow(held_ref[here, panel:], factors[:, :columns], PLAIN)
            result[n] = trailing_ref[here, :] - (both[:, :columns] + (both[:, columns:] + rest))
            store(n).start()

        @pl.loop(0, tiles)
        def _(n):
            store(n).wait()

    return kernel_call(
        kernel, (trailing, held, *weights), 6 * rows * panel * columns, 4 * rows * columns, 4 * rows * columns + GRANT,
        in_specs=[WHOLE] * (2 + chunks), out_specs=HBM, out_shape=outside(rows, columns),
        scratch_shapes=[
            pltpu.VMEM((tiles, tile, columns), jnp.float32),
            pltpu.VMEM((panel, 2 * columns), jnp.bfloat16),
            pltpu.SemaphoreType.DMA((tiles,)),
        ],
    )


def combine(level, current, received, pair, order, full=False, settled=None, updated=None):
    columns = current[0].shape[1]
    count, covered = len(current), sum(array.shape[0] for array in current)
    width = current[-1].shape[0]
    panel = pair[0].shape[1]
    last = updated is not None

    def kernel(*refs):
        current_refs, received_refs, refs = refs[:count], refs[count : 2 * count], refs[2 * count :]
        pair_refs, refs = refs[: len(pair)], refs[len(pair) :]
        if settled is not None:
            settled_ref, *refs = refs
        if last:
            _, out_ref, vectors, factor, result, sem = refs
        elif full:
            result, chunk_ref, vectors, factor = refs
        else:
            chunk_ref, vectors, factor = refs
        short, half = panel // len(order), len(order) // 2
        for n, mask in enumerate(order):
            to = pl.multiple_of((lax.axis_index("col") ^ mask) * short, short)
            part, m = pair_refs[n // half], n % half
            vectors[pl.ds(to, short), :] = part[2 * m * short : (2 * m + 1) * short, :]
            factor[pl.ds(to, short), :] = part[(2 * m + 1) * short : (2 * m + 2) * short, :]
        role = role_of(level)
        mine = jnp.concatenate([ref[...] for ref in current_refs], 0)
        other = jnp.concatenate([ref[...] for ref in received_refs], 0)
        leads = role == 1
        lower, upper = jnp.where(leads, mine, other), jnp.where(leads, other, mine)
        both = lower + product(vectors[:covered, :covered], upper, ROWS)
        taken = factor[:covered, :covered] if full else factor[:covered, covered - width : covered]
        weights = product(taken, both, ROWS)
        if full:
            @pl.when(role == 0)
            def _():
                result[...] = mine if settled is None else settled_ref[...]

            @pl.when(role == 1)
            def _():
                result[...] = lower - weights

            @pl.when(role == 2)
            def _():
                result[...] = upper - product(vectors[...], weights, PLAIN)

        if not last:
            chunk_ref[...] = lower[covered - width :] - weights[weights.shape[0] - width :]
        else:
            store = pltpu.make_async_copy(result, out_ref.at[pl.ds(0, covered)], sem.at[0])
            store.start()
            store.wait()

    optional = tuple(array for array in (settled, updated) if array is not None)
    arguments = (*current, *received, *pair, *optional)
    chunk, every = out(width, columns), out(covered, columns)
    return kernel_call(
        kernel, arguments, 18 * covered * panel * columns, 16 * covered * columns,
        in_specs=[WHOLE] * (len(arguments) - last) + [HBM] * last,
        out_specs=HBM if last else [WHOLE] * 2 if full else WHOLE,
        out_shape=outside(*updated.shape) if last else [every, chunk] if full else chunk,
        scratch_shapes=[pltpu.VMEM((panel, panel), jnp.float32)] * 2
        + ([pltpu.VMEM((covered, columns), jnp.float32), pltpu.SemaphoreType.DMA((1,))] if last else []),
        input_output_aliases={len(arguments) - 1: 0} if last else {},
    )


def gathered(parts, bits):
    if len(parts) == 2:
        core, wide, high = bits
        far = wide ^ high
        (upper, lower), cut = parts, parts[0].shape[0]
        near_a, near_b = exchanged(upper, wide), exchanged(lower, high)
        rest_b, rest_a = exchanged(lower, wide), exchanged(upper, high)
        steps = [
            [(0, 0, upper), (0, cut, lower)],
            [(wide, 0, near_a), (high, cut, near_b)],
            [(wide, cut, rest_b), (high, 0, rest_a)],
            [(far, 0, exchanged(near_a, high)), (far, cut, exchanged(near_b, wide))],
        ]
        across = [[(mask ^ core, offset, exchanged(array, core)) for mask, offset, array in step] for step in steps]
        return [steps[0] + across[0], steps[1] + across[1], steps[2] + across[2], steps[3], across[3]]
    blocks = [(0, 0, parts[0])]
    steps = [blocks]
    for bit in reversed(bits):
        steps.append([(mask ^ bit, 0, exchanged(block, bit)) for mask, _, block in blocks])
        blocks = blocks + steps[-1]
    return steps


def doubled(array, masks):
    order = [0]
    for n, mask in enumerate(masks):
        arrays = [array, exchanged(array, mask)]
        order = order + [m ^ mask for m in order]
        if n < len(masks) - 1:
            array = join(arrays)
    return arrays, order


def shards(trailing, leaf_vectors, leaf_factor, tree_vectors, tree_factor):
    down, across = lax.axis_size("row"), lax.axis_size("col")
    levels = down.bit_length() - 1
    bits = [1 << n for n in range(across.bit_length() - 1)]
    panel = leaf_factor.shape[1]
    tall, short = leaf_vectors.shape[0], leaf_factor.shape[0]
    rows = tall + short
    ranges = [(0, tall // 2), (tall // 2, rows)] if len(bits) == 3 else [(0, rows)]
    *parts, own = pack(leaf_vectors, leaf_factor, tree_vectors, tree_factor, ranges)
    trailing = load(trailing)

    pairs = []
    for level in range(levels):
        stride = 1 << level
        sent = lax.ppermute(own, "row", [(k + stride, k) for k in range(0, down, 2 * stride)])
        pair, order = doubled(pick(level, own, sent), bits[1:] + bits[:1])
        pairs.append(pair)

    state = None
    steps = gathered(parts, bits)
    half = panel // 2
    for n, pieces in enumerate(steps):
        state = gram(pieces, trailing, tall, short, state, half if n == len(steps) - 1 else None)
    held, square, total, weights, top = state
    more_weights, more_top = weigh(half, panel, trailing[0], held, square, total, weights)
    updated = update(trailing[0], held, (weights, more_weights))
    tops = [top, more_top]
    current, settled = tops, None
    for level in range(levels):
        stride = 1 << level
        swap = [pair for k in range(0, down, 2 * stride) for pair in ((k + stride, k), (k + stride // 2, k + stride))]
        received = [lax.ppermute(array, "row", swap) for array in current]
        if level == levels - 1:
            return combine(level, current, received, pairs[level], order, True, settled, updated)
        ahead = [combine(level, current[: c + 1], received[: c + 1], pairs[level], order) for c in range(len(tops) - 1)]
        settled, chunk = combine(level, current, received, pairs[level], order, True, settled)
        current = ahead + [chunk]


def solution(mesh):
    placed = (
        P("row", "col"),
        P(("row", "col"), None),
        P(("row", "col"), None),
        P(("row", "col"), None),
        P(("row", "col"), None),
    )

    return jax.shard_map(shards, mesh=mesh, in_specs=placed, out_specs=P("row", "col"), check_vma=False)
```

profile of v0, /device:TPU:0, one launch (start us, length us, event | category | flops | bytes accessed | tf_op | source)
XLA Modules:
  0.0 70.5 jit_solution(13555114610683528994)
XLA Ops:
  0.0 1.1 %shard_map.56 = (f32[256,256]{1,0:T(8,128)S(1)}, f32[288,256]{1,0:T(8,128)S(1)}, f32[64,256]{1,0:T(8,128)S(1)}) custom-call(f32[512,256]{1,0:T(8,128)} %vectors_ref.1, f32[32,256]{1,0:T(8,128)} %factor_ref.1, f32[32,256]{1,0:T(8,128)} %tree_vectors_ref.1, f32[32,256]{1,0:T(8,128)} %tree_factor_ref.1), custom_call_target="tpu_custom_call" | custom-call | bytes 1048576 | tf_op jit(solution)/shard_map/pallas_call | solution.py:64
  1.7 1.3 %collective-permute-start.15 = (f32[64,256]{1,0:T(8,128)S(1)}, f32[64,256]{1,0:T(8,128)S(1)}, u32[]{:S(2)}, u32[]{:S(2)}) collective-permute-start(f32[64,256]{1,0:T(8,128)S(1)} %get-tuple-element.50.own_ref), channel_id=1, source_target_pairs={{8,0},{24,16},{9,1},{25,17},{10,2},{26,18},{11,3},{27,19},{12,4},{... | collective-permute-start | bytes 196616 | tf_op jit(solution)/shard_map/ppermute | solution.py:368
  3.0 2.6 %collective-permute-start = (f32[256,256]{1,0:T(8,128)S(1)}, f32[256,256]{1,0:T(8,128)S(1)}, u32[]{:S(2)}, u32[]{:S(2)}) collective-permute-start(f32[256,256]{1,0:T(8,128)S(1)} %get-tuple-element.35.refs_0_), channel_id=1, source_target_pairs={{0,2},{1,3},{2,0},{3,1},{4,6},{5,7},{6,4},{7,5},{8,10},{9,11},{10,... | collective-permute-start | bytes 786440 | tf_op jit(solution)/shard_map/ppermute | solution.py:60
  5.5 1.3 %collective-permute-start.22 = (f32[64,256]{1,0:T(8,128)S(1)}, f32[64,256]{1,0:T(8,128)S(1)}, u32[]{:S(2)}, u32[]{:S(2)}) collective-permute-start(f32[64,256]{1,0:T(8,128)S(1)} %get-tuple-element.50.own_ref), channel_id=1, source_target_pairs={{16,0},{17,1},{18,2},{19,3},{20,4},{21,5},{22,6},{23,7}} | collective-permute-start | bytes 196616 | tf_op jit(solution)/shard_map/ppermute | solution.py:368
  6.8 1.6 %collective-permute-start.7 = (f32[256,256]{1,0:T(8,128)S(1)}, f32[256,256]{1,0:T(8,128)S(1)}, u32[]{:S(2)}, u32[]{:S(2)}) collective-permute-start(f32[256,256]{1,0:T(8,128)S(1)} %get-tuple-element.35.refs_0_), channel_id=1, source_target_pairs={{0,4},{1,5},{2,6},{3,7},{4,0},{5,1},{6,2},{7,3},{8,12},{9,13},{10,... | collective-permute-start | bytes 786440 | tf_op jit(solution)/shard_map/ppermute | solution.py:60
  8.4 2.2 %collective-permute-start.3 = (f32[288,256]{1,0:T(8,128)S(1)}, f32[288,256]{1,0:T(8,128)S(1)}, u32[]{:S(2)}, u32[]{:S(2)}) collective-permute-start(f32[288,256]{1,0:T(8,128)S(1)} %get-tuple-element.36.refs_1_), channel_id=1, source_target_pairs={{0,4},{1,5},{2,6},{3,7},{4,0},{5,1},{6,2},{7,3},{8,12},{9,13},{10,... | collective-permute-start | bytes 884744 | tf_op jit(solution)/shard_map/ppermute | solution.py:60
  10.6 2.0 %collective-permute-done.22.sent_ref = f32[64,256]{1,0:T(8,128)S(1)} collective-permute-done((f32[64,256]{1,0:T(8,128)S(1)}, f32[64,256]{1,0:T(8,128)S(1)}, u32[]{:S(2)}, u32[]{:S(2)}) %collective-permute-start.22) | collective-permute-done | bytes 65568 | tf_op jit(solution)/shard_map/ppermute | solution.py:368
  12.8 4.0 %collective-permute-done.16.refs_1_ = f32[64,256]{1,0:T(8,128)S(1)} collective-permute-done((f32[64,256]{1,0:T(8,128)S(1)}, f32[64,256]{1,0:T(8,128)S(1)}, u32[]{:S(2)}, u32[]{:S(2)}) %collective-permute-start.16) | collective-permute-done | bytes 65568 | tf_op jit(solution)/shard_map/ppermute | solution.py:60
  17.1 1.9 %collective-permute-start.17 = (f32[128,256]{1,0:T(8,128)S(1)}, f32[128,256]{1,0:T(8,128)S(1)}, u32[]{:S(2)}, u32[]{:S(2)}) collective-permute-start(f32[128,256]{1,0:T(8,128)S(1)} %shard_map.63.refs_0_), channel_id=1, source_target_pairs={{0,4},{1,5},{2,6},{3,7},{4,0},{5,1},{6,2},{7,3},{8,12},{9,13},{10,... | collective-permute-start | bytes 393224 | tf_op jit(solution)/shard_map/ppermute | solution.py:60
  19.0 3.4 %collective-permute-done.3.refs_1_ = f32[288,256]{1,0:T(8,128)S(1)} collective-permute-done((f32[288,256]{1,0:T(8,128)S(1)}, f32[288,256]{1,0:T(8,128)S(1)}, u32[]{:S(2)}, u32[]{:S(2)}) %collective-permute-start.3) | collective-permute-done | bytes 294944 | tf_op jit(solution)/shard_map/ppermute | solution.py:60
  22.4 2.0 %collective-permute-done.17.refs_1_ = f32[128,256]{1,0:T(8,128)S(1)} collective-permute-done((f32[128,256]{1,0:T(8,128)S(1)}, f32[128,256]{1,0:T(8,128)S(1)}, u32[]{:S(2)}, u32[]{:S(2)}) %collective-permute-start.17) | collective-permute-done | bytes 131104 | tf_op jit(solution)/shard_map/ppermute | solution.py:60
  24.4 1.5 %collective-permute-start.1 = (f32[256,256]{1,0:T(8,128)S(1)}, f32[256,256]{1,0:T(8,128)S(1)}, u32[]{:S(2)}, u32[]{:S(2)}) collective-permute-start(f32[256,256]{1,0:T(8,128)S(1)} %collective-permute-done.refs_0_), channel_id=1, source_target_pairs={{0,4},{1,5},{2,6},{3,7},{4,0},{5,1},{6,2},{7,3},{8,12},{9,13},{10,... | collective-permute-start | bytes 786440 | tf_op jit(solution)/shard_map/ppermute | solution.py:60
  26.0 0.8 %collective-permute-done.6.refs_0_ = f32[288,256]{1,0:T(8,128)S(1)} collective-permute-done((f32[288,256]{1,0:T(8,128)S(1)}, f32[288,256]{1,0:T(8,128)S(1)}, u32[]{:S(2)}, u32[]{:S(2)}) %collective-permute-start.6) | collective-permute-done | bytes 294944 | tf_op jit(solution)/shard_map/ppermute | solution.py:60
  27.2 5.3 %collective-permute-done.4.refs_1_ = f32[288,256]{1,0:T(8,128)S(1)} collective-permute-done((f32[288,256]{1,0:T(8,128)S(1)}, f32[288,256]{1,0:T(8,128)S(1)}, u32[]{:S(2)}, u32[]{:S(2)}) %collective-permute-start.4) | collective-permute-done | bytes 294944 | tf_op jit(solution)/shard_map/ppermute | solution.py:60
  32.6 3.0 %shard_map.55 = (f32[4096,384]{1,0:T(8,128)S(1)}, bf16[4096,384]{1,0:T(8,128)(2,1)S(1)}, bf16[4096,384]{1,0:T(8,128)(2,1)S(1)}) custom-call(f32[4096,384]{1,0:T(8,128)} %array_ref.1), custom_call_target="tpu_custom_call" | custom-call | bytes 18874368 | tf_op jit(solution)/shard_map/pallas_call | solution.py:64
  36.2 1.3 %shard_map.57 = (bf16[4096,512]{1,0:T(8,128)(2,1)S(1)}, f32[256,256]{1,0:T(8,128)S(1)}, f32[256,384]{1,0:T(8,128)S(1)}) custom-call(f32[4096,384]{1,0:T(8,128)S(1)} %get-tuple-element.32.whole_ref.trailing_ref, bf16[4096,384]{1,0:T(8,128)(2,1)S(1)} %get-tuple-element.33.high_ref, bf16[4096,384]{1,0:T(8,128)(2,1)S(1)} %get-tuple-element.34.lower_ref, ...), custom_call_target="tpu_custom_call" | custom-call | flops 855638016 | bytes 2228224 | tf_op jit(solution)/shard_map/pallas_call | solution.py:64
  37.8 1.3 %shard_map.58 = (bf16[4096,512]{1,0:T(8,128)(2,1)S(1)}, f32[256,256]{1,0:T(8,128)S(1)}, f32[256,384]{1,0:T(8,128)S(1)}) custom-call(f32[4096,384]{1,0:T(8,128)S(1)} %get-tuple-element.32.whole_ref.trailing_ref, bf16[4096,384]{1,0:T(8,128)(2,1)S(1)} %get-tuple-element.33.high_ref, ...), custom_call_target="tpu_custom_call", output_to_operand_aliasing={{0}: (7, {}), {1}: (8, {})} | custom-call | flops 855638016 | bytes 2228224 | tf_op jit(solution)/shard_map/pallas_call | solution.py:64
  39.2 1.3 %shard_map.59 = (bf16[4096,512]{1,0:T(8,128)(2,1)S(1)}, f32[256,256]{1,0:T(8,128)S(1)}, f32[256,384]{1,0:T(8,128)S(1)}) custom-call(f32[4096,384]{1,0:T(8,128)S(1)} %get-tuple-element.32.whole_ref.trailing_ref, bf16[4096,384]{1,0:T(8,128)(2,1)S(1)} %get-tuple-element.33.high_ref, ...), custom_call_target="tpu_custom_call", output_to_operand_aliasing={{0}: (7, {}), {1}: (8, {})} | custom-call | flops 855638016 | bytes 2228224 | tf_op jit(solution)/shard_map/pallas_call | solution.py:64
  40.5 0.7 %shard_map.60 = (bf16[4096,512]{1,0:T(8,128)(2,1)S(1)}, f32[256,256]{1,0:T(8,128)S(1)}, f32[256,384]{1,0:T(8,128)S(1)}) custom-call(f32[4096,384]{1,0:T(8,128)S(1)} %get-tuple-element.32.whole_ref.trailing_ref, bf16[4096,384]{1,0:T(8,128)(2,1)S(1)} %get-tuple-element.33.high_ref, ...), custom_call_target="tpu_custom_call", output_to_operand_aliasing={{0}: (5, {}), {1}: (6, {})} | custom-call | flops 427819008 | bytes 1114112 | tf_op jit(solution)/shard_map/pallas_call | solution.py:64
  41.3 1.2 %shard_map.61 = (bf16[4096,512]{1,0:T(8,128)(2,1)S(1)}, f32[256,256]{1,0:T(8,128)S(1)}, f32[256,384]{1,0:T(8,128)S(1)}, f32[128,384]{1,0:T(8,128)S(1)}, f32[128,384]{1,0:T(8,128)S(1)}) custom-call(f32[4096,384]{1,0:T(8,128)S(1)} %get-tuple-element.32.whole_ref.trailing_ref, ...), custom_call_target="tpu_custom_call", output_to_operand_aliasing={{0}: (5, {}), {1}: (6, {})} | custom-call | flops 427819008 | bytes 1114112 | tf_op jit(solution)/shard_map/pallas_call | solution.py:64
  43.1 0.9 %collective-permute-start.19 = (f32[128,384]{1,0:T(8,128)S(1)}, f32[128,384]{1,0:T(8,128)S(1)}, u32[]{:S(2)}, u32[]{:S(2)}) collective-permute-start(f32[128,384]{1,0:T(8,128)S(1)} %get-tuple-element.55.refs_1_), channel_id=1, source_target_pairs={{8,0},{0,8},{24,16},{16,24},{9,1},{1,9},{25,17},{17,25},{10,2},{2,... | collective-permute-start | bytes 589832 | tf_op jit(solution)/shard_map/ppermute | solution.py:385
  44.0 1.2 %collective-permute-start.14 = (f32[128,384]{1,0:T(8,128)S(1)}, f32[128,384]{1,0:T(8,128)S(1)}, u32[]{:S(2)}, u32[]{:S(2)}) collective-permute-start(f32[128,384]{1,0:T(8,128)S(1)} %get-tuple-element.49.refs_0_), channel_id=1, source_target_pairs={{8,0},{0,8},{24,16},{16,24},{9,1},{1,9},{25,17},{17,25},{10,2},{2,... | collective-permute-start | bytes 589832 | tf_op jit(solution)/shard_map/ppermute | solution.py:385
  45.2 1.8 %collective-permute-start.24 = (f32[128,256]{1,0:T(8,128)S(1)}, f32[128,256]{1,0:T(8,128)S(1)}, u32[]{:S(2)}, u32[]{:S(2)}) collective-permute-start(f32[128,256]{1,0:T(8,128)S(1)} %shard_map.69.refs_0_), channel_id=1, source_target_pairs={{0,4},{1,5},{2,6},{3,7},{4,0},{5,1},{6,2},{7,3},{8,12},{9,13},{10,... | collective-permute-start | bytes 393224 | tf_op jit(solution)/shard_map/ppermute | solution.py:60
  47.0 3.6 %collective-permute-done.24.refs_1_ = f32[128,256]{1,0:T(8,128)S(1)} collective-permute-done((f32[128,256]{1,0:T(8,128)S(1)}, f32[128,256]{1,0:T(8,128)S(1)}, u32[]{:S(2)}, u32[]{:S(2)}) %collective-permute-start.24) | collective-permute-done | bytes 131104 | tf_op jit(solution)/shard_map/ppermute | solution.py:60
  50.9 3.7 %collective-permute-done.14.refs_1_.refs_2_ = f32[128,384]{1,0:T(8,128)S(1)} collective-permute-done((f32[128,384]{1,0:T(8,128)S(1)}, f32[128,384]{1,0:T(8,128)S(1)}, u32[]{:S(2)}, u32[]{:S(2)}) %collective-permute-start.14) | collective-permute-done | bytes 196640 | tf_op jit(solution)/shard_map/ppermute | solution.py:385
  54.7 0.9 %shard_map.67 = (f32[256,384]{1,0:T(8,128)S(1)}, f32[128,384]{1,0:T(8,128)S(1)}) custom-call(f32[128,384]{1,0:T(8,128)S(1)} %get-tuple-element.49.refs_0_, f32[128,384]{1,0:T(8,128)S(1)} %get-tuple-element.55.refs_1_, f32[128,384]{1,0:T(8,128)S(1)} %collective-permute-done.14.refs_1_.refs_2_, f32[128,384]{1,0:T(8,128)S(1)} %collective-permute-done.19.refs_3_, ...), custom_call_target="tpu_custom_call" | custom-call | flops 452984832 | bytes 1572864 | tf_op jit(solution)/shard_map/pallas_call | solution.py:64
  55.5 1.3 %collective-permute-start.21 = (f32[128,384]{1,0:T(8,128)S(1)}, f32[128,384]{1,0:T(8,128)S(1)}, u32[]{:S(2)}, u32[]{:S(2)}) collective-permute-start(f32[128,384]{1,0:T(8,128)S(1)} %get-tuple-element.56.refs_1_), channel_id=1, source_target_pairs={{16,0},{8,16},{17,1},{9,17},{18,2},{10,18},{19,3},{11,19},{20,4},{... | collective-permute-start | bytes 589832 | tf_op jit(solution)/shard_map/ppermute | solution.py:385
  57.4 1.3 %collective-permute-start.20 = (f32[128,384]{1,0:T(8,128)S(1)}, f32[128,384]{1,0:T(8,128)S(1)}, u32[]{:S(2)}, u32[]{:S(2)}) collective-permute-start(f32[128,384]{1,0:T(8,128)S(1)} %shard_map.65.refs_0_), channel_id=1, source_target_pairs={{16,0},{8,16},{17,1},{9,17},{18,2},{10,18},{19,3},{11,19},{20,4},{... | collective-permute-start | bytes 589832 | tf_op jit(solution)/shard_map/ppermute | solution.py:385
  58.7 4.6 %shard_map.71.refs_7_ = f32[4096,384]{1,0:T(8,128)} custom-call(f32[4096,384]{1,0:T(8,128)S(1)} %get-tuple-element.32.whole_ref.trailing_ref, bf16[4096,512]{1,0:T(8,128)(2,1)S(1)} %get-tuple-element.51.held_ref, f32[128,384]{1,0:T(8,128)S(1)} %get-tuple-element.54.before_ref.refs_0_, f32[128,384]{1,0:T(8,128)S(1)} %get-tuple-element.58.refs_1_), custom_call_target="tpu_custom_call" | custom-call | flops 2415919104 | bytes 6291456 | tf_op jit(solution)/shard_map/pallas_call | solution.py:64
  63.4 2.7 %collective-permute-done.21.refs_3_ = f32[128,384]{1,0:T(8,128)S(1)} collective-permute-done((f32[128,384]{1,0:T(8,128)S(1)}, f32[128,384]{1,0:T(8,128)S(1)}, u32[]{:S(2)}, u32[]{:S(2)}) %collective-permute-start.21) | collective-permute-done | bytes 196640 | tf_op jit(solution)/shard_map/ppermute | solution.py:385
  66.1 2.9 %collective-permute-done.20.refs_2_ = f32[128,384]{1,0:T(8,128)S(1)} collective-permute-done((f32[128,384]{1,0:T(8,128)S(1)}, f32[128,384]{1,0:T(8,128)S(1)}, u32[]{:S(2)}, u32[]{:S(2)}) %collective-permute-start.20) | collective-permute-done | bytes 196640 | tf_op jit(solution)/shard_map/ppermute | solution.py:385
  69.0 1.6 %shard_map.72 = f32[4096,384]{1,0:T(8,128)} custom-call(f32[128,384]{1,0:T(8,128)S(1)} %shard_map.65.refs_0_, f32[128,384]{1,0:T(8,128)S(1)} %get-tuple-element.56.refs_1_, f32[128,384]{1,0:T(8,128)S(1)} %collective-permute-done.20.refs_2_, f32[128,384]{1,0:T(8,128)S(1)} %collective-permute-done.21.refs_3_, ...), custom_call_target="tpu_custom_call", output_to_operand_aliasing={{}: (7, {})} | custom-call | flops 452984832 | bytes 1572864 | tf_op jit(solution)/shard_map/pallas_call | solution.py:64
  (38 shorter events, 4.1 us)
Async XLA Ops:
  1.1 15.7 %collective-permute-start.12 = (f32[256,256]{1,0:T(8,128)S(1)}, f32[256,256]{1,0:T(8,128)S(1)}, u32[]{:S(2)}, u32[]{:S(2)}) collective-permute-start(f32[256,256]{1,0:T(8,128)S(1)} %get-tuple-element.35.refs_0_), channel_id=1, source_target_pairs={{0,1},{1,0},{2,3},{3,2},{4,5},{5,4},{6,7},{7,6},{8,9},{9,8},{10,11... | collective-permute-start | bytes 786440 | tf_op jit(solution)/shard_map/ppermute | solution.py:60
  1.7 6.7 %collective-permute-start.15 = (f32[64,256]{1,0:T(8,128)S(1)}, f32[64,256]{1,0:T(8,128)S(1)}, u32[]{:S(2)}, u32[]{:S(2)}) collective-permute-start(f32[64,256]{1,0:T(8,128)S(1)} %get-tuple-element.50.own_ref), channel_id=1, source_target_pairs={{8,0},{24,16},{9,1},{25,17},{10,2},{26,18},{11,3},{27,19},{12,4},{... | collective-permute-start | bytes 196616 | tf_op jit(solution)/shard_map/ppermute | solution.py:368
  3.0 14.1 %collective-permute-start = (f32[256,256]{1,0:T(8,128)S(1)}, f32[256,256]{1,0:T(8,128)S(1)}, u32[]{:S(2)}, u32[]{:S(2)}) collective-permute-start(f32[256,256]{1,0:T(8,128)S(1)} %get-tuple-element.35.refs_0_), channel_id=1, source_target_pairs={{0,2},{1,3},{2,0},{3,1},{4,6},{5,7},{6,4},{7,5},{8,10},{9,11},{10,... | collective-permute-start | bytes 786440 | tf_op jit(solution)/shard_map/ppermute | solution.py:60
  5.5 7.0 %collective-permute-start.22 = (f32[64,256]{1,0:T(8,128)S(1)}, f32[64,256]{1,0:T(8,128)S(1)}, u32[]{:S(2)}, u32[]{:S(2)}) collective-permute-start(f32[64,256]{1,0:T(8,128)S(1)} %get-tuple-element.50.own_ref), channel_id=1, source_target_pairs={{16,0},{17,1},{18,2},{19,3},{20,4},{21,5},{22,6},{23,7}} | collective-permute-start | bytes 196616 | tf_op jit(solution)/shard_map/ppermute | solution.py:368
  6.8 12.2 %collective-permute-start.7 = (f32[256,256]{1,0:T(8,128)S(1)}, f32[256,256]{1,0:T(8,128)S(1)}, u32[]{:S(2)}, u32[]{:S(2)}) collective-permute-start(f32[256,256]{1,0:T(8,128)S(1)} %get-tuple-element.35.refs_0_), channel_id=1, source_target_pairs={{0,4},{1,5},{2,6},{3,7},{4,0},{5,1},{6,2},{7,3},{8,12},{9,13},{10,... | collective-permute-start | bytes 786440 | tf_op jit(solution)/shard_map/ppermute | solution.py:60
  8.4 14.0 %collective-permute-start.3 = (f32[288,256]{1,0:T(8,128)S(1)}, f32[288,256]{1,0:T(8,128)S(1)}, u32[]{:S(2)}, u32[]{:S(2)}) collective-permute-start(f32[288,256]{1,0:T(8,128)S(1)} %get-tuple-element.36.refs_1_), channel_id=1, source_target_pairs={{0,4},{1,5},{2,6},{3,7},{4,0},{5,1},{6,2},{7,3},{8,12},{9,13},{10,... | collective-permute-start | bytes 884744 | tf_op jit(solution)/shard_map/ppermute | solution.py:60
  12.6 4.3 %collective-permute-start.16 = (f32[64,256]{1,0:T(8,128)S(1)}, f32[64,256]{1,0:T(8,128)S(1)}, u32[]{:S(2)}, u32[]{:S(2)}) collective-permute-start(f32[64,256]{1,0:T(8,128)S(1)} %shard_map.62.refs_0_), channel_id=1, source_target_pairs={{0,2},{1,3},{2,0},{3,1},{4,6},{5,7},{6,4},{7,5},{8,10},{9,11},{10,... | collective-permute-start | bytes 196616 | tf_op jit(solution)/shard_map/ppermute | solution.py:60
  16.8 9.1 %collective-permute-start.13 = (f32[288,256]{1,0:T(8,128)S(1)}, f32[288,256]{1,0:T(8,128)S(1)}, u32[]{:S(2)}, u32[]{:S(2)}) collective-permute-start(f32[288,256]{1,0:T(8,128)S(1)} %get-tuple-element.36.refs_1_), channel_id=1, source_target_pairs={{0,1},{1,0},{2,3},{3,2},{4,5},{5,4},{6,7},{7,6},{8,9},{9,8},{10,11... | collective-permute-start | bytes 884744 | tf_op jit(solution)/shard_map/ppermute | solution.py:60
  16.9 9.9 %collective-permute-start.6 = (f32[288,256]{1,0:T(8,128)S(1)}, f32[288,256]{1,0:T(8,128)S(1)}, u32[]{:S(2)}, u32[]{:S(2)}) collective-permute-start(f32[288,256]{1,0:T(8,128)S(1)} %get-tuple-element.36.refs_1_), channel_id=1, source_target_pairs={{0,2},{1,3},{2,0},{3,1},{4,6},{5,7},{6,4},{7,5},{8,10},{9,11},{10,... | collective-permute-start | bytes 884744 | tf_op jit(solution)/shard_map/ppermute | solution.py:60
  17.1 7.3 %collective-permute-start.17 = (f32[128,256]{1,0:T(8,128)S(1)}, f32[128,256]{1,0:T(8,128)S(1)}, u32[]{:S(2)}, u32[]{:S(2)}) collective-permute-start(f32[128,256]{1,0:T(8,128)S(1)} %shard_map.63.refs_0_), channel_id=1, source_target_pairs={{0,4},{1,5},{2,6},{3,7},{4,0},{5,1},{6,2},{7,3},{8,12},{9,13},{10,... | collective-permute-start | bytes 393224 | tf_op jit(solution)/shard_map/ppermute | solution.py:60
  19.0 7.7 %collective-permute-start.10 = (f32[256,256]{1,0:T(8,128)S(1)}, f32[256,256]{1,0:T(8,128)S(1)}, u32[]{:S(2)}, u32[]{:S(2)}) collective-permute-start(f32[256,256]{1,0:T(8,128)S(1)} %collective-permute-done.refs_0_), channel_id=1, source_target_pairs={{0,1},{1,0},{2,3},{3,2},{4,5},{5,4},{6,7},{7,6},{8,9},{9,8},{10,11... | collective-permute-start | bytes 786440 | tf_op jit(solution)/shard_map/ppermute | solution.py:60
  22.4 10.2 %collective-permute-start.4 = (f32[288,256]{1,0:T(8,128)S(1)}, f32[288,256]{1,0:T(8,128)S(1)}, u32[]{:S(2)}, u32[]{:S(2)}) collective-permute-start(f32[288,256]{1,0:T(8,128)S(1)} %collective-permute-done.3.refs_1_), channel_id=1, source_target_pairs={{0,2},{1,3},{2,0},{3,1},{4,6},{5,7},{6,4},{7,5},{8,10},{9,11},{10,... | collective-permute-start | bytes 884744 | tf_op jit(solution)/shard_map/ppermute | solution.py:60
  24.4 11.2 %collective-permute-start.1 = (f32[256,256]{1,0:T(8,128)S(1)}, f32[256,256]{1,0:T(8,128)S(1)}, u32[]{:S(2)}, u32[]{:S(2)}) collective-permute-start(f32[256,256]{1,0:T(8,128)S(1)} %collective-permute-done.refs_0_), channel_id=1, source_target_pairs={{0,4},{1,5},{2,6},{3,7},{4,0},{5,1},{6,2},{7,3},{8,12},{9,13},{10,... | collective-permute-start | bytes 786440 | tf_op jit(solution)/shard_map/ppermute | solution.py:60
  26.0 11.5 %collective-permute-start.11 = (f32[288,256]{1,0:T(8,128)S(1)}, f32[288,256]{1,0:T(8,128)S(1)}, u32[]{:S(2)}, u32[]{:S(2)}) collective-permute-start(f32[288,256]{1,0:T(8,128)S(1)} %collective-permute-done.3.refs_1_), channel_id=1, source_target_pairs={{0,1},{1,0},{2,3},{3,2},{4,5},{5,4},{6,7},{7,6},{8,9},{9,8},{10,11... | collective-permute-start | bytes 884744 | tf_op jit(solution)/shard_map/ppermute | solution.py:60
  26.7 12.5 %collective-permute-start.8 = (f32[288,256]{1,0:T(8,128)S(1)}, f32[288,256]{1,0:T(8,128)S(1)}, u32[]{:S(2)}, u32[]{:S(2)}) collective-permute-start(f32[288,256]{1,0:T(8,128)S(1)} %collective-permute-done.6.refs_0_), channel_id=1, source_target_pairs={{0,1},{1,0},{2,3},{3,2},{4,5},{5,4},{6,7},{7,6},{8,9},{9,8},{10,11... | collective-permute-start | bytes 884744 | tf_op jit(solution)/shard_map/ppermute | solution.py:60
  26.7 12.4 %collective-permute-start.9 = (f32[256,256]{1,0:T(8,128)S(1)}, f32[256,256]{1,0:T(8,128)S(1)}, u32[]{:S(2)}, u32[]{:S(2)}) collective-permute-start(f32[256,256]{1,0:T(8,128)S(1)} %collective-permute-done.7.refs_1_), channel_id=1, source_target_pairs={{0,1},{1,0},{2,3},{3,2},{4,5},{5,4},{6,7},{7,6},{8,9},{9,8},{10,11... | collective-permute-start | bytes 786440 | tf_op jit(solution)/shard_map/ppermute | solution.py:60
  32.6 8.7 %collective-permute-start.5 = (f32[288,256]{1,0:T(8,128)S(1)}, f32[288,256]{1,0:T(8,128)S(1)}, u32[]{:S(2)}, u32[]{:S(2)}) collective-permute-start(f32[288,256]{1,0:T(8,128)S(1)} %collective-permute-done.4.refs_1_), channel_id=1, source_target_pairs={{0,1},{1,0},{2,3},{3,2},{4,5},{5,4},{6,7},{7,6},{8,9},{9,8},{10,11... | collective-permute-start | bytes 884744 | tf_op jit(solution)/shard_map/ppermute | solution.py:60
  35.6 5.6 %collective-permute-start.2 = (f32[256,256]{1,0:T(8,128)S(1)}, f32[256,256]{1,0:T(8,128)S(1)}, u32[]{:S(2)}, u32[]{:S(2)}) collective-permute-start(f32[256,256]{1,0:T(8,128)S(1)} %collective-permute-done.1.refs_0_), channel_id=1, source_target_pairs={{0,1},{1,0},{2,3},{3,2},{4,5},{5,4},{6,7},{7,6},{8,9},{9,8},{10,11... | collective-permute-start | bytes 786440 | tf_op jit(solution)/shard_map/ppermute | solution.py:60
  37.5 7.7 %collective-permute-start.23 = (f32[64,256]{1,0:T(8,128)S(1)}, f32[64,256]{1,0:T(8,128)S(1)}, u32[]{:S(2)}, u32[]{:S(2)}) collective-permute-start(f32[64,256]{1,0:T(8,128)S(1)} %shard_map.68.refs_0_), channel_id=1, source_target_pairs={{0,2},{1,3},{2,0},{3,1},{4,6},{5,7},{6,4},{7,5},{8,10},{9,11},{10,... | collective-permute-start | bytes 196616 | tf_op jit(solution)/shard_map/ppermute | solution.py:60
  39.1 11.6 %collective-permute-start.18 = (f32[256,256]{1,0:T(8,128)S(1)}, f32[256,256]{1,0:T(8,128)S(1)}, u32[]{:S(2)}, u32[]{:S(2)}) collective-permute-start(f32[256,256]{1,0:T(8,128)S(1)} %shard_map.64.refs_2_.refs_4_), channel_id=1, source_target_pairs={{0,1},{1,0},{2,3},{3,2},{4,5},{5,4},{6,7},{7,6},{8,9},{9,8},{10,11... | collective-permute-start | bytes 786440 | tf_op jit(solution)/shard_map/ppermute | solution.py:60
  43.1 7.8 %collective-permute-start.19 = (f32[128,384]{1,0:T(8,128)S(1)}, f32[128,384]{1,0:T(8,128)S(1)}, u32[]{:S(2)}, u32[]{:S(2)}) collective-permute-start(f32[128,384]{1,0:T(8,128)S(1)} %get-tuple-element.55.refs_1_), channel_id=1, source_target_pairs={{8,0},{0,8},{24,16},{16,24},{9,1},{1,9},{25,17},{17,25},{10,2},{2,... | collective-permute-start | bytes 589832 | tf_op jit(solution)/shard_map/ppermute | solution.py:385
  44.0 10.6 %collective-permute-start.14 = (f32[128,384]{1,0:T(8,128)S(1)}, f32[128,384]{1,0:T(8,128)S(1)}, u32[]{:S(2)}, u32[]{:S(2)}) collective-permute-start(f32[128,384]{1,0:T(8,128)S(1)} %get-tuple-element.49.refs_0_), channel_id=1, source_target_pairs={{8,0},{0,8},{24,16},{16,24},{9,1},{1,9},{25,17},{17,25},{10,2},{2,... | collective-permute-start | bytes 589832 | tf_op jit(solution)/shard_map/ppermute | solution.py:385
  45.2 5.4 %collective-permute-start.24 = (f32[128,256]{1,0:T(8,128)S(1)}, f32[128,256]{1,0:T(8,128)S(1)}, u32[]{:S(2)}, u32[]{:S(2)}) collective-permute-start(f32[128,256]{1,0:T(8,128)S(1)} %shard_map.69.refs_0_), channel_id=1, source_target_pairs={{0,4},{1,5},{2,6},{3,7},{4,0},{5,1},{6,2},{7,3},{8,12},{9,13},{10,... | collective-permute-start | bytes 393224 | tf_op jit(solution)/shard_map/ppermute | solution.py:60
  50.6 12.7 %collective-permute-start.25 = (f32[256,256]{1,0:T(8,128)S(1)}, f32[256,256]{1,0:T(8,128)S(1)}, u32[]{:S(2)}, u32[]{:S(2)}) collective-permute-start(f32[256,256]{1,0:T(8,128)S(1)} %shard_map.70.refs_4_), channel_id=1, source_target_pairs={{0,1},{1,0},{2,3},{3,2},{4,5},{5,4},{6,7},{7,6},{8,9},{9,8},{10,11... | collective-permute-start | bytes 786440 | tf_op jit(solution)/shard_map/ppermute | solution.py:60
  55.5 10.6 %collective-permute-start.21 = (f32[128,384]{1,0:T(8,128)S(1)}, f32[128,384]{1,0:T(8,128)S(1)}, u32[]{:S(2)}, u32[]{:S(2)}) collective-permute-start(f32[128,384]{1,0:T(8,128)S(1)} %get-tuple-element.56.refs_1_), channel_id=1, source_target_pairs={{16,0},{8,16},{17,1},{9,17},{18,2},{10,18},{19,3},{11,19},{20,4},{... | collective-permute-start | bytes 589832 | tf_op jit(solution)/shard_map/ppermute | solution.py:385
  57.4 11.6 %collective-permute-start.20 = (f32[128,384]{1,0:T(8,128)S(1)}, f32[128,384]{1,0:T(8,128)S(1)}, u32[]{:S(2)}, u32[]{:S(2)}) collective-permute-start(f32[128,384]{1,0:T(8,128)S(1)} %shard_map.65.refs_0_), channel_id=1, source_target_pairs={{16,0},{8,16},{17,1},{9,17},{18,2},{10,18},{19,3},{11,19},{20,4},{... | collective-permute-start | bytes 589832 | tf_op jit(solution)/shard_map/ppermute | solution.py:385
where the time goes:
time: 70.8 us; the launch traced here: 70.5 us
  waiting for transfers between devices  30.7 us (43%)
  starting transfers between devices  21.4 us (30%)
  Pallas kernels  18.2 us (26%)
    ppermute x20, waiting for transfers between devices, exchanged(): lax.ppermute(array, 'col', [(i, i ^ mask) for i in range(lax.axis_size('c...  19.2 us
    pallas_call x18, Pallas kernels, kernel_call(): pl.pallas_call(kernel, compiler_params=pltpu.CompilerParams(vmem_limit_by...  18.2 us
    ppermute x20, starting transfers between devices, exchanged(): lax.ppermute(array, 'col', [(i, i ^ mask) for i in range(lax.axis_size('c...  14.2 us
    ppermute x4, waiting for transfers between devices, shards(): received = [lax.ppermute(array, 'row', swap) for array in current]  9.52 us
    ppermute x4, starting transfers between devices, shards(): received = [lax.ppermute(array, 'row', swap) for array in current]  4.68 us
    ppermute x2, starting transfers between devices, shards(): lax.ppermute(own, 'row', [(k + stride, k) for k in range(0, down, 2 * str...  2.56 us
    ppermute x2, waiting for transfers between devices, shards(): lax.ppermute(own, 'row', [(k + stride, k) for k in range(0, down, 2 * str...  1.99 us
  transfers between devices with their start and end apart: 26, of which 11 were waited for; matrix products, arithmetic and copies ran while one was open for 0% of the time, Pallas kernels for 22%

commit v1 on v0

--- a/solution.py
+++ b/solution.py
@@ -143,17 +143,20 @@
     )
 
 
-def gram(pieces, trailing, tall, short, state, top=None):
+def gram(pieces, trailing, tall, short, state, part, span=None, before=None):
     whole, _, _ = trailing
     width, columns = pieces[0][2].shape[1], whole.shape[1]
     rows = whole.shape[0]
     count, begins = len(pieces), state is None
+    first, last = part
 
     def kernel(whole_ref, high_ref, lower_ref, *refs):
         piece_refs, refs = refs[:count], refs[count:]
         total_of = None
         if not begins:
-            total_of, refs = refs[2][...], refs[3:]
+            total_of, refs = refs[2][first:last, :], refs[3:]
+        if before is not None:
+            before_ref, *refs = refs
         held_ref, square_ref, total_ref, *refs = refs
         place = lax.axis_index("col")
         for (mask, offset, array), ref in zip(pieces, piece_refs):
@@ -161,29 +164,33 @@
             block = place ^ mask
             upper = min(size, tall - offset)
             here = pl.ds(pl.multiple_of(block * tall + offset, math.gcd(tall, offset)), upper)
-            vectors = jnp.concatenate(halves(ref[:upper, :]), 1)
-            held_ref[here, :] = vectors
+            leads, trails = halves(ref[:upper, first:last])
+            held_ref[here, first:last] = leads
+            held_ref[here, width + first : width + last] = trails
+            vectors = jnp.concatenate([leads, trails], 1)
             term = narrow(vectors, high_ref[here, :], ROWS) + narrow(vectors, lower_ref[here, :], ROWS)
-            term = term[:width] + term[width:]
+            term = term[: last - first] + term[last - first :]
             total_of = term if total_of is None else total_of + term
             if upper < size:
                 there = pl.ds(pl.multiple_of(block * short, short), short)
-                square_ref[there, :] = ref[upper:, :]
-        total_ref[...] = total_of
-        if top is not None:
-            leading(0, top, whole_ref, held_ref, square_ref, total_of, None, *refs)
+                square_ref[there, first:last] = ref[upper:, first:last]
+        total_ref[first:last, :] = total_of
+        if span is not None:
+            weights = None if before is None else before_ref[...]
+            leading(*span, whole_ref, held_ref, square_ref, total_ref[: span[1], :], weights, *refs)
 
     arrays = [piece[2] for piece in pieces]
     taken = sum(array.shape[0] for array in arrays)
     states = () if begins else state
-    return kernel_call(
-        kernel, (*trailing, *arrays, *states),
-        8 * taken * width * columns, 8 * taken * width,
-        in_specs=[WHOLE] * (3 + count + len(states)),
-        out_specs=[WHOLE] * (3 if top is None else 5),
+    extra = () if before is None else (before,)
+    return kernel_call(
+        kernel, (*trailing, *arrays, *states, *extra),
+        8 * taken * (last - first) * columns, 8 * taken * (last - first),
+        in_specs=[WHOLE] * (3 + count + len(states) + len(extra)),
+        out_specs=[WHOLE] * (3 if span is None else 5),
         out_shape=[pltpu.VMEM((rows, 2 * width), jnp.bfloat16), out(width, width), out(width, columns)]
-        + ([] if top is None else [out(top, columns)] * 2),
-        input_output_aliases={} if begins else {3 + count: 0, 4 + count: 1},
+        + ([] if span is None else [out(span[1] - span[0], columns)] * 2),
+        input_output_aliases={} if begins else {3 + count + n: n for n in range(3)},
     )
 
 
@@ -195,18 +202,6 @@
         weights = jnp.concatenate([before, weights], 0)
     vectors = held_ref[low:high, :]
     top_ref[...] = whole_ref[low:high, :] - thrice(vectors[:, :high], vectors[:, width : width + high], *halves(weights))
-
-
-def weigh(low, high, trailing, held, square, total, before):
-    columns = trailing.shape[1]
-
-    def kernel(whole_ref, held_ref, square_ref, total_ref, before_ref, weights_ref, top_ref):
-        leading(low, high, whole_ref, held_ref, square_ref, total_ref[...], before_ref[...], weights_ref, top_ref)
-
-    return kernel_call(
-        kernel, (trailing, held, square, total, before), 6 * high * high * columns, 8 * high * columns,
-        in_specs=[WHOLE] * 5, out_specs=[WHOLE] * 2, out_shape=[out(high - low, columns)] * 2,
-    )
 
 
 def update(trailing, held, weights):
@@ -372,10 +367,12 @@
     state = None
     steps = gathered(parts, bits)
     half = panel // 2
-    for n, pieces in enumerate(steps):
-        state = gram(pieces, trailing, tall, short, state, half if n == len(steps) - 1 else None)
-    held, square, total, weights, top = state
-    more_weights, more_top = weigh(half, panel, trailing[0], held, square, total, weights)
+    left, right = (0, half), (half, panel)
+    for pieces in steps[:-1]:
+        state = gram(pieces, trailing, tall, short, state, (0, panel))
+    *state, weights, top = gram(steps[-1], trailing, tall, short, state, left, left)
+    *state, more_weights, more_top = gram(steps[-1], trailing, tall, short, state, right, right, weights)
+    held = state[0]
     updated = update(trailing[0], held, (weights, more_weights))
     tops = [top, more_top]
     current, settled = tops, None

time: 70.8 us -> 70.9 us (level)
  no operation moved by 1% of the time
where the time goes in v1:
time: 70.9 us; the launch traced here: 70.7 us
  waiting for transfers between devices  30.7 us (43%)
  starting transfers between devices  21.4 us (30%)
  Pallas kernels  18.4 us (26%)
    ppermute x20, waiting for transfers between devices, exchanged(): lax.ppermute(array, 'col', [(i, i ^ mask) for i in range(lax.axis_size('c...  19.2 us
    pallas_call x18, Pallas kernels, kernel_call(): pl.pallas_call(kernel, compiler_params=pltpu.CompilerParams(vmem_limit_by...  18.4 us
    ppermute x20, starting transfers between devices, exchanged(): lax.ppermute(array, 'col', [(i, i ^ mask) for i in range(lax.axis_size('c...  14.2 us
    ppermute x4, waiting for transfers between devices, shards(): received = [lax.ppermute(array, 'row', swap) for array in current]  9.52 us
    ppermute x4, starting transfers between devices, shards(): received = [lax.ppermute(array, 'row', swap) for array in current]  4.68 us
    ppermute x2, starting transfers between devices, shards(): lax.ppermute(own, 'row', [(k + stride, k) for k in range(0, down, 2 * str...  2.56 us
    ppermute x2, waiting for transfers between devices, shards(): lax.ppermute(own, 'row', [(k + stride, k) for k in range(0, down, 2 * str...  1.99 us
  transfers between devices with their start and end apart: 26, of which 11 were waited for; matrix products, arithmetic and copies ran while one was open for 0% of the time, Pallas kernels for 22%

profile of v1, /device:TPU:0, one launch (start us, length us, event | category | flops | bytes accessed | tf_op | source)
XLA Modules:
  0.0 70.7 jit_solution(9495634035949094125)
XLA Ops:
  0.0 1.1 %shard_map.56 = (f32[256,256]{1,0:T(8,128)S(1)}, f32[288,256]{1,0:T(8,128)S(1)}, f32[64,256]{1,0:T(8,128)S(1)}) custom-call(f32[512,256]{1,0:T(8,128)} %vectors_ref.1, f32[32,256]{1,0:T(8,128)} %factor_ref.1, f32[32,256]{1,0:T(8,128)} %tree_vectors_ref.1, f32[32,256]{1,0:T(8,128)} %tree_factor_ref.1), custom_call_target="tpu_custom_call" | custom-call | bytes 1048576 | tf_op jit(solution)/shard_map/pallas_call | solution.py:64
  1.7 1.3 %collective-permute-start.15 = (f32[64,256]{1,0:T(8,128)S(1)}, f32[64,256]{1,0:T(8,128)S(1)}, u32[]{:S(2)}, u32[]{:S(2)}) collective-permute-start(f32[64,256]{1,0:T(8,128)S(1)} %get-tuple-element.51.own_ref), channel_id=1, source_target_pairs={{8,0},{24,16},{9,1},{25,17},{10,2},{26,18},{11,3},{27,19},{12,4},{... | collective-permute-start | bytes 196616 | tf_op jit(solution)/shard_map/ppermute | solution.py:363
  3.0 2.6 %collective-permute-start = (f32[256,256]{1,0:T(8,128)S(1)}, f32[256,256]{1,0:T(8,128)S(1)}, u32[]{:S(2)}, u32[]{:S(2)}) collective-permute-start(f32[256,256]{1,0:T(8,128)S(1)} %get-tuple-element.36.refs_0_), channel_id=1, source_target_pairs={{0,2},{1,3},{2,0},{3,1},{4,6},{5,7},{6,4},{7,5},{8,10},{9,11},{10,... | collective-permute-start | bytes 786440 | tf_op jit(solution)/shard_map/ppermute | solution.py:60
  5.5 1.3 %collective-permute-start.22 = (f32[64,256]{1,0:T(8,128)S(1)}, f32[64,256]{1,0:T(8,128)S(1)}, u32[]{:S(2)}, u32[]{:S(2)}) collective-permute-start(f32[64,256]{1,0:T(8,128)S(1)} %get-tuple-element.51.own_ref), channel_id=1, source_target_pairs={{16,0},{17,1},{18,2},{19,3},{20,4},{21,5},{22,6},{23,7}} | collective-permute-start | bytes 196616 | tf_op jit(solution)/shard_map/ppermute | solution.py:363
  6.8 1.6 %collective-permute-start.7 = (f32[256,256]{1,0:T(8,128)S(1)}, f32[256,256]{1,0:T(8,128)S(1)}, u32[]{:S(2)}, u32[]{:S(2)}) collective-permute-start(f32[256,256]{1,0:T(8,128)S(1)} %get-tuple-element.36.refs_0_), channel_id=1, source_target_pairs={{0,4},{1,5},{2,6},{3,7},{4,0},{5,1},{6,2},{7,3},{8,12},{9,13},{10,... | collective-permute-start | bytes 786440 | tf_op jit(solution)/shard_map/ppermute | solution.py:60
  8.4 2.2 %collective-permute-start.3 = (f32[288,256]{1,0:T(8,128)S(1)}, f32[288,256]{1,0:T(8,128)S(1)}, u32[]{:S(2)}, u32[]{:S(2)}) collective-permute-start(f32[288,256]{1,0:T(8,128)S(1)} %get-tuple-element.37.refs_1_), channel_id=1, source_target_pairs={{0,4},{1,5},{2,6},{3,7},{4,0},{5,1},{6,2},{7,3},{8,12},{9,13},{10,... | collective-permute-start | bytes 884744 | tf_op jit(solution)/shard_map/ppermute | solution.py:60
  10.6 2.0 %collective-permute-done.22.sent_ref = f32[64,256]{1,0:T(8,128)S(1)} collective-permute-done((f32[64,256]{1,0:T(8,128)S(1)}, f32[64,256]{1,0:T(8,128)S(1)}, u32[]{:S(2)}, u32[]{:S(2)}) %collective-permute-start.22) | collective-permute-done | bytes 65568 | tf_op jit(solution)/shard_map/ppermute | solution.py:363
  12.8 4.0 %collective-permute-done.16.refs_1_ = f32[64,256]{1,0:T(8,128)S(1)} collective-permute-done((f32[64,256]{1,0:T(8,128)S(1)}, f32[64,256]{1,0:T(8,128)S(1)}, u32[]{:S(2)}, u32[]{:S(2)}) %collective-permute-start.16) | collective-permute-done | bytes 65568 | tf_op jit(solution)/shard_map/ppermute | solution.py:60
  17.1 1.9 %collective-permute-start.17 = (f32[128,256]{1,0:T(8,128)S(1)}, f32[128,256]{1,0:T(8,128)S(1)}, u32[]{:S(2)}, u32[]{:S(2)}) collective-permute-start(f32[128,256]{1,0:T(8,128)S(1)} %shard_map.63.refs_0_), channel_id=1, source_target_pairs={{0,4},{1,5},{2,6},{3,7},{4,0},{5,1},{6,2},{7,3},{8,12},{9,13},{10,... | collective-permute-start | bytes 393224 | tf_op jit(solution)/shard_map/ppermute | solution.py:60
  19.0 3.4 %collective-permute-done.3.refs_1_ = f32[288,256]{1,0:T(8,128)S(1)} collective-permute-done((f32[288,256]{1,0:T(8,128)S(1)}, f32[288,256]{1,0:T(8,128)S(1)}, u32[]{:S(2)}, u32[]{:S(2)}) %collective-permute-start.3) | collective-permute-done | bytes 294944 | tf_op jit(solution)/shard_map/ppermute | solution.py:60
  22.4 2.0 %collective-permute-done.17.refs_1_ = f32[128,256]{1,0:T(8,128)S(1)} collective-permute-done((f32[128,256]{1,0:T(8,128)S(1)}, f32[128,256]{1,0:T(8,128)S(1)}, u32[]{:S(2)}, u32[]{:S(2)}) %collective-permute-start.17) | collective-permute-done | bytes 131104 | tf_op jit(solution)/shard_map/ppermute | solution.py:60
  24.4 1.5 %collective-permute-start.1 = (f32[256,256]{1,0:T(8,128)S(1)}, f32[256,256]{1,0:T(8,128)S(1)}, u32[]{:S(2)}, u32[]{:S(2)}) collective-permute-start(f32[256,256]{1,0:T(8,128)S(1)} %collective-permute-done.refs_0_), channel_id=1, source_target_pairs={{0,4},{1,5},{2,6},{3,7},{4,0},{5,1},{6,2},{7,3},{8,12},{9,13},{10,... | collective-permute-start | bytes 786440 | tf_op jit(solution)/shard_map/ppermute | solution.py:60
  26.0 0.8 %collective-permute-done.6.refs_0_ = f32[288,256]{1,0:T(8,128)S(1)} collective-permute-done((f32[288,256]{1,0:T(8,128)S(1)}, f32[288,256]{1,0:T(8,128)S(1)}, u32[]{:S(2)}, u32[]{:S(2)}) %collective-permute-start.6) | collective-permute-done | bytes 294944 | tf_op jit(solution)/shard_map/ppermute | solution.py:60
  27.2 5.3 %collective-permute-done.4.refs_1_ = f32[288,256]{1,0:T(8,128)S(1)} collective-permute-done((f32[288,256]{1,0:T(8,128)S(1)}, f32[288,256]{1,0:T(8,128)S(1)}, u32[]{:S(2)}, u32[]{:S(2)}) %collective-permute-start.4) | collective-permute-done | bytes 294944 | tf_op jit(solution)/shard_map/ppermute | solution.py:60
  32.6 3.0 %shard_map.55 = (f32[4096,384]{1,0:T(8,128)S(1)}, bf16[4096,384]{1,0:T(8,128)(2,1)S(1)}, bf16[4096,384]{1,0:T(8,128)(2,1)S(1)}) custom-call(f32[4096,384]{1,0:T(8,128)} %array_ref.1), custom_call_target="tpu_custom_call" | custom-call | bytes 18874368 | tf_op jit(solution)/shard_map/pallas_call | solution.py:64
  36.2 1.3 %shard_map.57 = (bf16[4096,512]{1,0:T(8,128)(2,1)S(1)}, f32[256,256]{1,0:T(8,128)S(1)}, f32[256,384]{1,0:T(8,128)S(1)}) custom-call(f32[4096,384]{1,0:T(8,128)S(1)} %get-tuple-element.33.whole_ref.trailing_ref, bf16[4096,384]{1,0:T(8,128)(2,1)S(1)} %get-tuple-element.34.high_ref, bf16[4096,384]{1,0:T(8,128)(2,1)S(1)} %get-tuple-element.35.lower_ref, ...), custom_call_target="tpu_custom_call" | custom-call | flops 855638016 | bytes 2228224 | tf_op jit(solution)/shard_map/pallas_call | solution.py:64
  37.8 1.3 %shard_map.58 = (bf16[4096,512]{1,0:T(8,128)(2,1)S(1)}, f32[256,256]{1,0:T(8,128)S(1)}, f32[256,384]{1,0:T(8,128)S(1)}) custom-call(f32[4096,384]{1,0:T(8,128)S(1)} %get-tuple-element.33.whole_ref.trailing_ref, bf16[4096,384]{1,0:T(8,128)(2,1)S(1)} %get-tuple-element.34.high_ref, ...), custom_call_target="tpu_custom_call", output_to_operand_aliasing={{0}: (7, {}), {1}: (8, {}), {2}: (9, {})} | custom-call | flops 855638016 | bytes 2228224 | tf_op jit(solution)/shard_map/pallas_call | solution.py:64
  39.2 1.3 %shard_map.59 = (bf16[4096,512]{1,0:T(8,128)(2,1)S(1)}, f32[256,256]{1,0:T(8,128)S(1)}, f32[256,384]{1,0:T(8,128)S(1)}) custom-call(f32[4096,384]{1,0:T(8,128)S(1)} %get-tuple-element.33.whole_ref.trailing_ref, bf16[4096,384]{1,0:T(8,128)(2,1)S(1)} %get-tuple-element.34.high_ref, ...), custom_call_target="tpu_custom_call", output_to_operand_aliasing={{0}: (7, {}), {1}: (8, {}), {2}: (9, {})} | custom-call | flops 855638016 | bytes 2228224 | tf_op jit(solution)/shard_map/pallas_call | solution.py:64
  41.3 1.0 %shard_map.61 = (bf16[4096,512]{1,0:T(8,128)(2,1)S(1)}, f32[256,256]{1,0:T(8,128)S(1)}, f32[256,384]{1,0:T(8,128)S(1)}, f32[128,384]{1,0:T(8,128)S(1)}, f32[128,384]{1,0:T(8,128)S(1)}) custom-call(f32[4096,384]{1,0:T(8,128)S(1)} %get-tuple-element.33.whole_ref.trailing_ref, ...), custom_call_target="tpu_custom_call", output_to_operand_aliasing={{0}: (5, {}), {1}: (6, {}), {2}: (7, {})} | custom-call | flops 213909504 | bytes 557056 | tf_op jit(solution)/shard_map/pallas_call | solution.py:64
  42.3 1.0 %shard_map.66 = (bf16[4096,512]{1,0:T(8,128)(2,1)S(1)}, f32[256,256]{1,0:T(8,128)S(1)}, f32[256,384]{1,0:T(8,128)S(1)}, f32[128,384]{1,0:T(8,128)S(1)}, f32[128,384]{1,0:T(8,128)S(1)}) custom-call(f32[4096,384]{1,0:T(8,128)S(1)} %get-tuple-element.33.whole_ref.trailing_ref, ...), custom_call_target="tpu_custom_call", output_to_operand_aliasing={{0}: (5, {}), {1}: (6, {}), {2}: (7, {})} | custom-call | flops 213909504 | bytes 557056 | tf_op jit(solution)/shard_map/pallas_call | solution.py:64
  43.3 0.9 %collective-permute-start.19 = (f32[128,384]{1,0:T(8,128)S(1)}, f32[128,384]{1,0:T(8,128)S(1)}, u32[]{:S(2)}, u32[]{:S(2)}) collective-permute-start(f32[128,384]{1,0:T(8,128)S(1)} %get-tuple-element.56.refs_1_), channel_id=1, source_target_pairs={{8,0},{0,8},{24,16},{16,24},{9,1},{1,9},{25,17},{17,25},{10,2},{2,... | collective-permute-start | bytes 589832 | tf_op jit(solution)/shard_map/ppermute | solution.py:382
  44.2 1.2 %collective-permute-start.14 = (f32[128,384]{1,0:T(8,128)S(1)}, f32[128,384]{1,0:T(8,128)S(1)}, u32[]{:S(2)}, u32[]{:S(2)}) collective-permute-start(f32[128,384]{1,0:T(8,128)S(1)} %get-tuple-element.50.refs_0_), channel_id=1, source_target_pairs={{8,0},{0,8},{24,16},{16,24},{9,1},{1,9},{25,17},{17,25},{10,2},{2,... | collective-permute-start | bytes 589832 | tf_op jit(solution)/shard_map/ppermute | solution.py:382
  45.4 1.8 %collective-permute-start.24 = (f32[128,256]{1,0:T(8,128)S(1)}, f32[128,256]{1,0:T(8,128)S(1)}, u32[]{:S(2)}, u32[]{:S(2)}) collective-permute-start(f32[128,256]{1,0:T(8,128)S(1)} %shard_map.69.refs_0_), channel_id=1, source_target_pairs={{0,4},{1,5},{2,6},{3,7},{4,0},{5,1},{6,2},{7,3},{8,12},{9,13},{10,... | collective-permute-start | bytes 393224 | tf_op jit(solution)/shard_map/ppermute | solution.py:60
  47.2 3.6 %collective-permute-done.24.refs_1_ = f32[128,256]{1,0:T(8,128)S(1)} collective-permute-done((f32[128,256]{1,0:T(8,128)S(1)}, f32[128,256]{1,0:T(8,128)S(1)}, u32[]{:S(2)}, u32[]{:S(2)}) %collective-permute-start.24) | collective-permute-done | bytes 131104 | tf_op jit(solution)/shard_map/ppermute | solution.py:60
  51.1 3.7 %collective-permute-done.14.refs_1_.refs_2_ = f32[128,384]{1,0:T(8,128)S(1)} collective-permute-done((f32[128,384]{1,0:T(8,128)S(1)}, f32[128,384]{1,0:T(8,128)S(1)}, u32[]{:S(2)}, u32[]{:S(2)}) %collective-permute-start.14) | collective-permute-done | bytes 196640 | tf_op jit(solution)/shard_map/ppermute | solution.py:382
  54.8 0.9 %shard_map.67 = (f32[256,384]{1,0:T(8,128)S(1)}, f32[128,384]{1,0:T(8,128)S(1)}) custom-call(f32[128,384]{1,0:T(8,128)S(1)} %get-tuple-element.50.refs_0_, f32[128,384]{1,0:T(8,128)S(1)} %get-tuple-element.56.refs_1_, f32[128,384]{1,0:T(8,128)S(1)} %collective-permute-done.14.refs_1_.refs_2_, f32[128,384]{1,0:T(8,128)S(1)} %collective-permute-done.19.refs_3_, ...), custom_call_target="tpu_custom_call" | custom-call | flops 452984832 | bytes 1572864 | tf_op jit(solution)/shard_map/pallas_call | solution.py:64
  55.7 1.3 %collective-permute-start.21 = (f32[128,384]{1,0:T(8,128)S(1)}, f32[128,384]{1,0:T(8,128)S(1)}, u32[]{:S(2)}, u32[]{:S(2)}) collective-permute-start(f32[128,384]{1,0:T(8,128)S(1)} %get-tuple-element.57.refs_1_), channel_id=1, source_target_pairs={{16,0},{8,16},{17,1},{9,17},{18,2},{10,18},{19,3},{11,19},{20,4},{... | collective-permute-start | bytes 589832 | tf_op jit(solution)/shard_map/ppermute | solution.py:382
  57.6 1.3 %collective-permute-start.20 = (f32[128,384]{1,0:T(8,128)S(1)}, f32[128,384]{1,0:T(8,128)S(1)}, u32[]{:S(2)}, u32[]{:S(2)}) collective-permute-start(f32[128,384]{1,0:T(8,128)S(1)} %shard_map.65.refs_0_), channel_id=1, source_target_pairs={{16,0},{8,16},{17,1},{9,17},{18,2},{10,18},{19,3},{11,19},{20,4},{... | collective-permute-start | bytes 589832 | tf_op jit(solution)/shard_map/ppermute | solution.py:382
  58.9 4.6 %shard_map.71.refs_7_ = f32[4096,384]{1,0:T(8,128)} custom-call(f32[4096,384]{1,0:T(8,128)S(1)} %get-tuple-element.33.whole_ref.trailing_ref, bf16[4096,512]{1,0:T(8,128)(2,1)S(1)} %get-tuple-element.59.held_ref, f32[128,384]{1,0:T(8,128)S(1)} %get-tuple-element.55.refs_5_.refs_0_, f32[128,384]{1,0:T(8,128)S(1)} %get-tuple-element.60.refs_1_), custom_call_target="tpu_custom_call" | custom-call | flops 2415919104 | bytes 6291456 | tf_op jit(solution)/shard_map/pallas_call | solution.py:64
  63.5 2.7 %collective-permute-done.21.refs_3_ = f32[128,384]{1,0:T(8,128)S(1)} collective-permute-done((f32[128,384]{1,0:T(8,128)S(1)}, f32[128,384]{1,0:T(8,128)S(1)}, u32[]{:S(2)}, u32[]{:S(2)}) %collective-permute-start.21) | collective-permute-done | bytes 196640 | tf_op jit(solution)/shard_map/ppermute | solution.py:382
  66.3 2.9 %collective-permute-done.20.refs_2_ = f32[128,384]{1,0:T(8,128)S(1)} collective-permute-done((f32[128,384]{1,0:T(8,128)S(1)}, f32[128,384]{1,0:T(8,128)S(1)}, u32[]{:S(2)}, u32[]{:S(2)}) %collective-permute-start.20) | collective-permute-done | bytes 196640 | tf_op jit(solution)/shard_map/ppermute | solution.py:382
  69.1 1.6 %shard_map.72 = f32[4096,384]{1,0:T(8,128)} custom-call(f32[128,384]{1,0:T(8,128)S(1)} %shard_map.65.refs_0_, f32[128,384]{1,0:T(8,128)S(1)} %get-tuple-element.57.refs_1_, f32[128,384]{1,0:T(8,128)S(1)} %collective-permute-done.20.refs_2_, f32[128,384]{1,0:T(8,128)S(1)} %collective-permute-done.21.refs_3_, ...), custom_call_target="tpu_custom_call", output_to_operand_aliasing={{}: (7, {})} | custom-call | flops 452984832 | bytes 1572864 | tf_op jit(solution)/shard_map/pallas_call | solution.py:64
  (38 shorter events, 4.3 us)
Async XLA Ops:
  1.1 15.7 %collective-permute-start.12 = (f32[256,256]{1,0:T(8,128)S(1)}, f32[256,256]{1,0:T(8,128)S(1)}, u32[]{:S(2)}, u32[]{:S(2)}) collective-permute-start(f32[256,256]{1,0:T(8,128)S(1)} %get-tuple-element.36.refs_0_), channel_id=1, source_target_pairs={{0,1},{1,0},{2,3},{3,2},{4,5},{5,4},{6,7},{7,6},{8,9},{9,8},{10,11... | collective-permute-start | bytes 786440 | tf_op jit(solution)/shard_map/ppermute | solution.py:60
  1.7 6.7 %collective-permute-start.15 = (f32[64,256]{1,0:T(8,128)S(1)}, f32[64,256]{1,0:T(8,128)S(1)}, u32[]{:S(2)}, u32[]{:S(2)}) collective-permute-start(f32[64,256]{1,0:T(8,128)S(1)} %get-tuple-element.51.own_ref), channel_id=1, source_target_pairs={{8,0},{24,16},{9,1},{25,17},{10,2},{26,18},{11,3},{27,19},{12,4},{... | collective-permute-start | bytes 196616 | tf_op jit(solution)/shard_map/ppermute | solution.py:363
  3.0 14.1 %collective-permute-start = (f32[256,256]{1,0:T(8,128)S(1)}, f32[256,256]{1,0:T(8,128)S(1)}, u32[]{:S(2)}, u32[]{:S(2)}) collective-permute-start(f32[256,256]{1,0:T(8,128)S(1)} %get-tuple-element.36.refs_0_), channel_id=1, source_target_pairs={{0,2},{1,3},{2,0},{3,1},{4,6},{5,7},{6,4},{7,5},{8,10},{9,11},{10,... | collective-permute-start | bytes 786440 | tf_op jit(solution)/shard_map/ppermute | solution.py:60
  5.5 7.0 %collective-permute-start.22 = (f32[64,256]{1,0:T(8,128)S(1)}, f32[64,256]{1,0:T(8,128)S(1)}, u32[]{:S(2)}, u32[]{:S(2)}) collective-permute-start(f32[64,256]{1,0:T(8,128)S(1)} %get-tuple-element.51.own_ref), channel_id=1, source_target_pairs={{16,0},{17,1},{18,2},{19,3},{20,4},{21,5},{22,6},{23,7}} | collective-permute-start | bytes 196616 | tf_op jit(solution)/shard_map/ppermute | solution.py:363
  6.8 12.2 %collective-permute-start.7 = (f32[256,256]{1,0:T(8,128)S(1)}, f32[256,256]{1,0:T(8,128)S(1)}, u32[]{:S(2)}, u32[]{:S(2)}) collective-permute-start(f32[256,256]{1,0:T(8,128)S(1)} %get-tuple-element.36.refs_0_), channel_id=1, source_target_pairs={{0,4},{1,5},{2,6},{3,7},{4,0},{5,1},{6,2},{7,3},{8,12},{9,13},{10,... | collective-permute-start | bytes 786440 | tf_op jit(solution)/shard_map/ppermute | solution.py:60
  8.4 14.0 %collective-permute-start.3 = (f32[288,256]{1,0:T(8,128)S(1)}, f32[288,256]{1,0:T(8,128)S(1)}, u32[]{:S(2)}, u32[]{:S(2)}) collective-permute-start(f32[288,256]{1,0:T(8,128)S(1)} %get-tuple-element.37.refs_1_), channel_id=1, source_target_pairs={{0,4},{1,5},{2,6},{3,7},{4,0},{5,1},{6,2},{7,3},{8,12},{9,13},{10,... | collective-permute-start | bytes 884744 | tf_op jit(solution)/shard_map/ppermute | solution.py:60
  12.6 4.3 %collective-permute-start.16 = (f32[64,256]{1,0:T(8,128)S(1)}, f32[64,256]{1,0:T(8,128)S(1)}, u32[]{:S(2)}, u32[]{:S(2)}) collective-permute-start(f32[64,256]{1,0:T(8,128)S(1)} %shard_map.62.refs_0_), channel_id=1, source_target_pairs={{0,2},{1,3},{2,0},{3,1},{4,6},{5,7},{6,4},{7,5},{8,10},{9,11},{10,... | collective-permute-start | bytes 196616 | tf_op jit(solution)/shard_map/ppermute | solution.py:60
  16.8 9.1 %collective-permute-start.13 = (f32[288,256]{1,0:T(8,128)S(1)}, f32[288,256]{1,0:T(8,128)S(1)}, u32[]{:S(2)}, u32[]{:S(2)}) collective-permute-start(f32[288,256]{1,0:T(8,128)S(1)} %get-tuple-element.37.refs_1_), channel_id=1, source_target_pairs={{0,1},{1,0},{2,3},{3,2},{4,5},{5,4},{6,7},{7,6},{8,9},{9,8},{10,11... | collective-permute-start | bytes 884744 | tf_op jit(solution)/shard_map/ppermute | solution.py:60
  16.9 9.9 %collective-permute-start.6 = (f32[288,256]{1,0:T(8,128)S(1)}, f32[288,256]{1,0:T(8,128)S(1)}, u32[]{:S(2)}, u32[]{:S(2)}) collective-permute-start(f32[288,256]{1,0:T(8,128)S(1)} %get-tuple-element.37.refs_1_), channel_id=1, source_target_pairs={{0,2},{1,3},{2,0},{3,1},{4,6},{5,7},{6,4},{7,5},{8,10},{9,11},{10,... | collective-permute-start | bytes 884744 | tf_op jit(solution)/shard_map/ppermute | solution.py:60
  17.1 7.3 %collective-permute-start.17 = (f32[128,256]{1,0:T(8,128)S(1)}, f32[128,256]{1,0:T(8,128)S(1)}, u32[]{:S(2)}, u32[]{:S(2)}) collective-permute-start(f32[128,256]{1,0:T(8,128)S(1)} %shard_map.63.refs_0_), channel_id=1, source_target_pairs={{0,4},{1,5},{2,6},{3,7},{4,0},{5,1},{6,2},{7,3},{8,12},{9,13},{10,... | collective-permute-start | bytes 393224 | tf_op jit(solution)/shard_map/ppermute | solution.py:60
  19.0 7.7 %collective-permute-start.10 = (f32[256,256]{1,0:T(8,128)S(1)}, f32[256,256]{1,0:T(8,128)S(1)}, u32[]{:S(2)}, u32[]{:S(2)}) collective-permute-start(f32[256,256]{1,0:T(8,128)S(1)} %collective-permute-done.refs_0_), channel_id=1, source_target_pairs={{0,1},{1,0},{2,3},{3,2},{4,5},{5,4},{6,7},{7,6},{8,9},{9,8},{10,11... | collective-permute-start | bytes 786440 | tf_op jit(solution)/shard_map/ppermute | solution.py:60
  22.4 10.2 %collective-permute-start.4 = (f32[288,256]{1,0:T(8,128)S(1)}, f32[288,256]{1,0:T(8,128)S(1)}, u32[]{:S(2)}, u32[]{:S(2)}) collective-permute-start(f32[288,256]{1,0:T(8,128)S(1)} %collective-permute-done.3.refs_1_), channel_id=1, source_target_pairs={{0,2},{1,3},{2,0},{3,1},{4,6},{5,7},{6,4},{7,5},{8,10},{9,11},{10,... | collective-permute-start | bytes 884744 | tf_op jit(solution)/shard_map/ppermute | solution.py:60
  24.4 11.2 %collective-permute-start.1 = (f32[256,256]{1,0:T(8,128)S(1)}, f32[256,256]{1,0:T(8,128)S(1)}, u32[]{:S(2)}, u32[]{:S(2)}) collective-permute-start(f32[256,256]{1,0:T(8,128)S(1)} %collective-permute-done.refs_0_), channel_id=1, source_target_pairs={{0,4},{1,5},{2,6},{3,7},{4,0},{5,1},{6,2},{7,3},{8,12},{9,13},{10,... | collective-permute-start | bytes 786440 | tf_op jit(solution)/shard_map/ppermute | solution.py:60
  26.0 11.5 %collective-permute-start.11 = (f32[288,256]{1,0:T(8,128)S(1)}, f32[288,256]{1,0:T(8,128)S(1)}, u32[]{:S(2)}, u32[]{:S(2)}) collective-permute-start(f32[288,256]{1,0:T(8,128)S(1)} %collective-permute-done.3.refs_1_), channel_id=1, source_target_pairs={{0,1},{1,0},{2,3},{3,2},{4,5},{5,4},{6,7},{7,6},{8,9},{9,8},{10,11... | collective-permute-start | bytes 884744 | tf_op jit(solution)/shard_map/ppermute | solution.py:60
  26.7 12.5 %collective-permute-start.8 = (f32[288,256]{1,0:T(8,128)S(1)}, f32[288,256]{1,0:T(8,128)S(1)}, u32[]{:S(2)}, u32[]{:S(2)}) collective-permute-start(f32[288,256]{1,0:T(8,128)S(1)} %collective-permute-done.6.refs_0_), channel_id=1, source_target_pairs={{0,1},{1,0},{2,3},{3,2},{4,5},{5,4},{6,7},{7,6},{8,9},{9,8},{10,11... | collective-permute-start | bytes 884744 | tf_op jit(solution)/shard_map/ppermute | solution.py:60
  26.7 12.4 %collective-permute-start.9 = (f32[256,256]{1,0:T(8,128)S(1)}, f32[256,256]{1,0:T(8,128)S(1)}, u32[]{:S(2)}, u32[]{:S(2)}) collective-permute-start(f32[256,256]{1,0:T(8,128)S(1)} %collective-permute-done.7.refs_1_), channel_id=1, source_target_pairs={{0,1},{1,0},{2,3},{3,2},{4,5},{5,4},{6,7},{7,6},{8,9},{9,8},{10,11... | collective-permute-start | bytes 786440 | tf_op jit(solution)/shard_map/ppermute | solution.py:60
  32.6 8.7 %collective-permute-start.5 = (f32[288,256]{1,0:T(8,128)S(1)}, f32[288,256]{1,0:T(8,128)S(1)}, u32[]{:S(2)}, u32[]{:S(2)}) collective-permute-start(f32[288,256]{1,0:T(8,128)S(1)} %collective-permute-done.4.refs_1_), channel_id=1, source_target_pairs={{0,1},{1,0},{2,3},{3,2},{4,5},{5,4},{6,7},{7,6},{8,9},{9,8},{10,11... | collective-permute-start | bytes 884744 | tf_op jit(solution)/shard_map/ppermute | solution.py:60
  35.6 5.6 %collective-permute-start.2 = (f32[256,256]{1,0:T(8,128)S(1)}, f32[256,256]{1,0:T(8,128)S(1)}, u32[]{:S(2)}, u32[]{:S(2)}) collective-permute-start(f32[256,256]{1,0:T(8,128)S(1)} %collective-permute-done.1.refs_0_), channel_id=1, source_target_pairs={{0,1},{1,0},{2,3},{3,2},{4,5},{5,4},{6,7},{7,6},{8,9},{9,8},{10,11... | collective-permute-start | bytes 786440 | tf_op jit(solution)/shard_map/ppermute | solution.py:60
  37.5 7.9 %collective-permute-start.23 = (f32[64,256]{1,0:T(8,128)S(1)}, f32[64,256]{1,0:T(8,128)S(1)}, u32[]{:S(2)}, u32[]{:S(2)}) collective-permute-start(f32[64,256]{1,0:T(8,128)S(1)} %shard_map.68.refs_0_), channel_id=1, source_target_pairs={{0,2},{1,3},{2,0},{3,1},{4,6},{5,7},{6,4},{7,5},{8,10},{9,11},{10,... | collective-permute-start | bytes 196616 | tf_op jit(solution)/shard_map/ppermute | solution.py:60
  39.1 11.8 %collective-permute-start.18 = (f32[256,256]{1,0:T(8,128)S(1)}, f32[256,256]{1,0:T(8,128)S(1)}, u32[]{:S(2)}, u32[]{:S(2)}) collective-permute-start(f32[256,256]{1,0:T(8,128)S(1)} %shard_map.64.refs_2_.refs_4_), channel_id=1, source_target_pairs={{0,1},{1,0},{2,3},{3,2},{4,5},{5,4},{6,7},{7,6},{8,9},{9,8},{10,11... | collective-permute-start | bytes 786440 | tf_op jit(solution)/shard_map/ppermute | solution.py:60
  43.3 7.8 %collective-permute-start.19 = (f32[128,384]{1,0:T(8,128)S(1)}, f32[128,384]{1,0:T(8,128)S(1)}, u32[]{:S(2)}, u32[]{:S(2)}) collective-permute-start(f32[128,384]{1,0:T(8,128)S(1)} %get-tuple-element.56.refs_1_), channel_id=1, source_target_pairs={{8,0},{0,8},{24,16},{16,24},{9,1},{1,9},{25,17},{17,25},{10,2},{2,... | collective-permute-start | bytes 589832 | tf_op jit(solution)/shard_map/ppermute | solution.py:382
  44.2 10.6 %collective-permute-start.14 = (f32[128,384]{1,0:T(8,128)S(1)}, f32[128,384]{1,0:T(8,128)S(1)}, u32[]{:S(2)}, u32[]{:S(2)}) collective-permute-start(f32[128,384]{1,0:T(8,128)S(1)} %get-tuple-element.50.refs_0_), channel_id=1, source_target_pairs={{8,0},{0,8},{24,16},{16,24},{9,1},{1,9},{25,17},{17,25},{10,2},{2,... | collective-permute-start | bytes 589832 | tf_op jit(solution)/shard_map/ppermute | solution.py:382
  45.4 5.4 %collective-permute-start.24 = (f32[128,256]{1,0:T(8,128)S(1)}, f32[128,256]{1,0:T(8,128)S(1)}, u32[]{:S(2)}, u32[]{:S(2)}) collective-permute-start(f32[128,256]{1,0:T(8,128)S(1)} %shard_map.69.refs_0_), channel_id=1, source_target_pairs={{0,4},{1,5},{2,6},{3,7},{4,0},{5,1},{6,2},{7,3},{8,12},{9,13},{10,... | collective-permute-start | bytes 393224 | tf_op jit(solution)/shard_map/ppermute | solution.py:60
  50.8 12.7 %collective-permute-start.25 = (f32[256,256]{1,0:T(8,128)S(1)}, f32[256,256]{1,0:T(8,128)S(1)}, u32[]{:S(2)}, u32[]{:S(2)}) collective-permute-start(f32[256,256]{1,0:T(8,128)S(1)} %shard_map.70.refs_4_), channel_id=1, source_target_pairs={{0,1},{1,0},{2,3},{3,2},{4,5},{5,4},{6,7},{7,6},{8,9},{9,8},{10,11... | collective-permute-start | bytes 786440 | tf_op jit(solution)/shard_map/ppermute | solution.py:60
  55.7 10.6 %collective-permute-start.21 = (f32[128,384]{1,0:T(8,128)S(1)}, f32[128,384]{1,0:T(8,128)S(1)}, u32[]{:S(2)}, u32[]{:S(2)}) collective-permute-start(f32[128,384]{1,0:T(8,128)S(1)} %get-tuple-element.57.refs_1_), channel_id=1, source_target_pairs={{16,0},{8,16},{17,1},{9,17},{18,2},{10,18},{19,3},{11,19},{20,4},{... | collective-permute-start | bytes 589832 | tf_op jit(solution)/shard_map/ppermute | solution.py:382
  57.6 11.6 %collective-permute-start.20 = (f32[128,384]{1,0:T(8,128)S(1)}, f32[128,384]{1,0:T(8,128)S(1)}, u32[]{:S(2)}, u32[]{:S(2)}) collective-permute-start(f32[128,384]{1,0:T(8,128)S(1)} %shard_map.65.refs_0_), channel_id=1, source_target_pairs={{16,0},{8,16},{17,1},{9,17},{18,2},{10,18},{19,3},{11,19},{20,4},{... | collective-permute-start | bytes 589832 | tf_op jit(solution)/shard_map/ppermute | solution.py:382
